TPU v7x, 32 devices: a whole 2x2x4 slice. The times are simulated.
32 devices in a mesh: dp: 8 (over z, core), tensor: 4 (over y, x).
Axes of the slice: x: 2, y: 2, z: 4, core: 2. Of those that a mesh axis runs over, the one named last changes fastest.
Arguments:
- tokens: bfloat16 [8192, 1024], P('dp'), may hold values from -6 to 6
- segment_ids: int32 [8, 1024], P('dp'), may hold values from 0 to 7, never falling along the last dimension, each value on 1 to 512 neighbouring positions
- ln1_gain: float32 [1024], replicated, may hold values from 0.1 to 1.9
- ln1_shift: float32 [1024], replicated, may hold values from -1.75 to 1.75
- w_qkv: bfloat16 [3, 1024, 1024], P(None, None, 'tensor'), may hold values from -2 to 2
- b_qv: float32 [2, 1024], P(None, 'tensor'), may hold values from -3 to 3
- w_out: bfloat16 [1024, 1024], P('tensor'), may hold values from -0.75 to 0.75
- b_out: float32 [1024], replicated, may hold values from -3 to 3
- ln2_gain: float32 [1024], replicated, may hold values from 0.1 to 1.9
- ln2_shift: float32 [1024], replicated, may hold values from -1.75 to 1.75
- w_up: bfloat16 [1024, 4096], P(None, 'tensor'), may hold values from -0.1875 to 0.1875
- b_up: float32 [4096], P('tensor'), may hold values from -3 to 3
- w_down: bfloat16 [4096, 1024], P('tensor'), may hold values from -0.09375 to 0.09375
- b_down: float32 [1024], replicated, may hold values from -3 to 3
- d_out: bfloat16 [8192, 1024], P('dp'), may hold values from -6 to 6
Outputs:
- output: bfloat16 [8192, 1024], P('dp')
- d_tokens: bfloat16 [8192, 1024], P('dp')
- g_ln1_gain: float32 [1024], replicated
- g_ln1_shift: float32 [1024], replicated
- g_qkv: float32 [3, 1024, 1024], P(None, None, 'tensor')
- g_qv_bias: float32 [2, 1024], P(None, 'tensor')
- g_out: float32 [1024, 1024], P('tensor')
- g_out_bias: float32 [1024], replicated
- g_ln2_gain: float32 [1024], replicated
- g_ln2_shift: float32 [1024], replicated
- g_up: float32 [1024, 4096], P(None, 'tensor')
- g_up_bias: float32 [4096], P('tensor')
- g_down: float32 [4096, 1024], P('tensor')
- g_down_bias: float32 [1024], replicated
Inputs may be any that keep to these rules, and one draw needn't show every extreme that they name: `segment_ids`: each row numbers its packed sequences from 0 without falling; every sequence has 1 to 512 tokens and one has exactly 512.
All inputs are finite; a program needn't handle non-finite values.
Results may differ from a plain program's by a relative error of at most 0.019.
Values may be sent and summed in bfloat16 or wider, within the bound.
A program may use at most 192 MiB of HBM per device.

v0:
```python
import jax
import jax.numpy as jnp
from jax import lax
from jax.sharding import PartitionSpec as P

HD = 64
epsilon = 1e-05
gelu_coef = 0.7978845608028654


def gelu_value(values):
    inner = jnp.tanh(gelu_coef * (values + 0.044715 * values * values * values))
    return 0.5 * values * (1.0 + inner)


def gelu_slope(values):
    inner = jnp.tanh(gelu_coef * (values + 0.044715 * values * values * values))
    return 0.5 * (1.0 + inner) + 0.5 * values * (1.0 - inner * inner) * gelu_coef * (
        1.0 + 3.0 * 0.044715 * values * values
    )


def norm_parts(values):
    centered = values - jnp.mean(values, axis=-1, keepdims=True)
    inverse = lax.rsqrt(jnp.mean(centered * centered, axis=-1, keepdims=True) + epsilon)
    return (centered * inverse, inverse)


def norm_back(grad_in, normed, inverse, gain):
    scaled = grad_in * gain
    return inverse * (
        scaled
        - jnp.mean(scaled, axis=-1, keepdims=True)
        - normed * jnp.mean(scaled * normed, axis=-1, keepdims=True)
    )


def row_slice(values):
    row_count = values.shape[0] // lax.axis_size("tensor")
    return lax.dynamic_slice_in_dim(values, lax.axis_index("tensor") * row_count, row_count, 0)


def block_mask(seg_query, seg_keys, first_row):
    shape_here = (seg_query.shape[0], seg_keys.shape[0])
    query_pos = first_row + lax.broadcasted_iota(jnp.int32, shape_here, 0)
    key_pos = lax.broadcasted_iota(jnp.int32, shape_here, 1)
    return (seg_query[:, None] == seg_keys[None, :]) & (key_pos <= query_pos)


def attention_forward(query_heads, key_heads, value_heads, seg_row):
    length = query_heads.shape[1]
    block_rows = 512
    scale = query_heads.shape[2] ** (-0.5)
    outputs = []
    totals = []
    for first_row in range(0, length, block_rows):
        rows_q = query_heads[:, first_row : first_row + block_rows]
        scores = (
            jnp.einsum("hqd,hkd->hqk", rows_q, key_heads, preferred_element_type=jnp.float32)
            * scale
        )
        allowed = block_mask(seg_row[first_row : first_row + block_rows], seg_row, first_row)
        scores = jnp.where(allowed[None], scores, -jnp.inf)
        maximum = jnp.max(scores, axis=-1, keepdims=True)
        log_total = jnp.log(jnp.sum(jnp.exp(scores - maximum), axis=-1, keepdims=True)) + maximum
        weights_bf = jnp.exp(scores - log_total).astype(jnp.bfloat16)
        outputs.append(
            jnp.einsum(
                "hqk,hkd->hqd", weights_bf, value_heads, preferred_element_type=jnp.float32
            ).astype(jnp.bfloat16)
        )
        totals.append(log_total)
    return (jnp.concatenate(outputs, axis=1), jnp.concatenate(totals, axis=1))


def attention_backward(query_heads, key_heads, value_heads, seg_row, log_totals, grad_ctx):
    length = query_heads.shape[1]
    block_rows = 512
    scale = query_heads.shape[2] ** (-0.5)
    grad_keys = jnp.zeros(key_heads.shape, jnp.float32)
    grad_values = jnp.zeros(value_heads.shape, jnp.float32)
    grad_queries = []
    for first_row in range(0, length, block_rows):
        rows_q = query_heads[:, first_row : first_row + block_rows]
        scores = (
            jnp.einsum("hqd,hkd->hqk", rows_q, key_heads, preferred_element_type=jnp.float32)
            * scale
        )
        allowed = block_mask(seg_row[first_row : first_row + block_rows], seg_row, first_row)
        scores = jnp.where(allowed[None], scores, -jnp.inf)
        weights = jnp.exp(scores - log_totals[:, first_row : first_row + block_rows])
        weights_bf = weights.astype(jnp.bfloat16)
        grad_rows_ctx = grad_ctx[:, first_row : first_row + block_rows]
        grad_weights = jnp.einsum(
            "hqd,hkd->hqk", grad_rows_ctx, value_heads, preferred_element_type=jnp.float32
        )
        inner_sum = jnp.sum(weights * grad_weights, axis=-1, keepdims=True)
        grad_scores = (weights * (grad_weights - inner_sum)).astype(jnp.bfloat16)
        grad_queries.append(
            (
                jnp.einsum(
                    "hqk,hkd->hqd", grad_scores, key_heads, preferred_element_type=jnp.float32
                )
                * scale
            ).astype(jnp.bfloat16)
        )
        grad_keys = (
            grad_keys
            + jnp.einsum("hqk,hqd->hkd", grad_scores, rows_q, preferred_element_type=jnp.float32)
            * scale
        )
        grad_values = grad_values + jnp.einsum(
            "hqk,hqd->hkd", weights_bf, grad_rows_ctx, preferred_element_type=jnp.float32
        )
    return (
        jnp.concatenate(grad_queries, axis=1),
        grad_keys.astype(jnp.bfloat16),
        grad_values.astype(jnp.bfloat16),
    )


def per_device(
    tokens,
    segment_ids,
    ln1_gain,
    ln1_shift,
    w_qkv,
    b_qv,
    w_out,
    b_out,
    ln2_gain,
    ln2_shift,
    w_up,
    b_up,
    w_down,
    b_down,
    d_out,
):
    seg_row = segment_ids[0]
    length = tokens.shape[0]
    local_width = w_qkv.shape[2]
    head_count = local_width // HD
    tokens_f = tokens.astype(jnp.float32)
    normed1, inverse1 = norm_parts(tokens_f)
    input1 = (normed1 * ln1_gain + ln1_shift).astype(jnp.bfloat16)
    projected = jnp.einsum("sd,ide->ise", input1, w_qkv, preferred_element_type=jnp.float32)
    bias_rows = jnp.stack([b_qv[0], jnp.zeros_like(b_qv[0]), b_qv[1]])
    projected = (projected + bias_rows[:, None, :]).astype(jnp.bfloat16)
    split_heads = projected.reshape(3, length, head_count, HD).transpose(0, 2, 1, 3)
    query_heads, key_heads, value_heads = (split_heads[0], split_heads[1], split_heads[2])
    context_heads, log_totals = attention_forward(query_heads, key_heads, value_heads, seg_row)
    context = context_heads.transpose(1, 0, 2).reshape(length, local_width)
    attn_part = jnp.dot(context, w_out, preferred_element_type=jnp.float32)
    attn_sum = lax.psum(attn_part.astype(jnp.bfloat16), "tensor").astype(jnp.float32)
    resid_mid = tokens_f + attn_sum + b_out
    normed2, inverse2 = norm_parts(resid_mid)
    input2 = (normed2 * ln2_gain + ln2_shift).astype(jnp.bfloat16)
    pre_act = jnp.dot(input2, w_up, preferred_element_type=jnp.float32) + b_up
    activated = gelu_value(pre_act).astype(jnp.bfloat16)
    mlp_part = jnp.dot(activated, w_down, preferred_element_type=jnp.float32)
    mlp_sum = lax.psum(mlp_part.astype(jnp.bfloat16), "tensor").astype(jnp.float32)
    output = (resid_mid + mlp_sum + b_down).astype(jnp.bfloat16)
    grad_out = d_out.astype(jnp.float32)
    grad_rows = row_slice(grad_out)
    g_down_bias = jnp.sum(grad_rows, axis=0)
    g_down = jnp.einsum("sf,sd->fd", activated, d_out, preferred_element_type=jnp.float32)
    grad_act = jnp.einsum("sd,fd->sf", d_out, w_down, preferred_element_type=jnp.float32)
    grad_pre = (grad_act * gelu_slope(pre_act)).astype(jnp.bfloat16)
    g_up = jnp.einsum("sd,sf->df", input2, grad_pre, preferred_element_type=jnp.float32)
    g_up_bias = jnp.sum(grad_pre.astype(jnp.float32), axis=0)
    normed_part = jnp.einsum("sf,df->sd", grad_pre, w_up, preferred_element_type=jnp.float32)
    normed_grad = lax.psum(normed_part.astype(jnp.bfloat16), "tensor").astype(jnp.float32)
    resid_grad = grad_out + norm_back(normed_grad, normed2, inverse2, ln2_gain)
    normed_grad_rows = row_slice(normed_grad)
    g_ln2_gain = jnp.sum(normed_grad_rows * row_slice(normed2), axis=0)
    g_ln2_shift = jnp.sum(normed_grad_rows, axis=0)
    g_out_bias = jnp.sum(row_slice(resid_grad), axis=0)
    resid_grad_bf = resid_grad.astype(jnp.bfloat16)
    g_out = jnp.einsum("sk,sd->kd", context, resid_grad_bf, preferred_element_type=jnp.float32)
    grad_context = jnp.einsum(
        "sd,kd->sk", resid_grad_bf, w_out, preferred_element_type=jnp.float32
    ).astype(jnp.bfloat16)
    grad_ctx_heads = grad_context.reshape(length, head_count, HD).transpose(1, 0, 2)
    grad_q, grad_k, grad_v = attention_backward(
        query_heads, key_heads, value_heads, seg_row, log_totals, grad_ctx_heads
    )
    grad_proj = (
        jnp.stack([grad_q, grad_k, grad_v]).transpose(0, 2, 1, 3).reshape(3, length, local_width)
    )
    g_qkv = jnp.einsum("sd,ise->ide", input1, grad_proj, preferred_element_type=jnp.float32)
    g_qv_bias = jnp.stack(
        [
            jnp.sum(grad_proj[0].astype(jnp.float32), axis=0),
            jnp.sum(grad_proj[2].astype(jnp.float32), axis=0),
        ]
    )
    input_part = jnp.einsum("ise,ide->sd", grad_proj, w_qkv, preferred_element_type=jnp.float32)
    input_grad = lax.psum(input_part.astype(jnp.bfloat16), "tensor").astype(jnp.float32)
    d_tokens = (resid_grad + norm_back(input_grad, normed1, inverse1, ln1_gain)).astype(
        jnp.bfloat16
    )
    input_grad_share = row_slice(input_grad)
    normed1_share = row_slice(normed1)
    g_ln1_gain = jnp.sum(input_grad_share * normed1_share, axis=0)
    g_ln1_shift = jnp.sum(input_grad_share, axis=0)
    g_qkv, g_qv_bias, g_out, g_up, g_up_bias, g_down = lax.psum(
        (g_qkv, g_qv_bias, g_out, g_up, g_up_bias, g_down), "dp"
    )
    g_ln1_gain, g_ln1_shift, g_out_bias, g_ln2_gain, g_ln2_shift, g_down_bias = lax.psum(
        (g_ln1_gain, g_ln1_shift, g_out_bias, g_ln2_gain, g_ln2_shift, g_down_bias),
        ("dp", "tensor"),
    )
    return (
        output,
        d_tokens,
        g_ln1_gain,
        g_ln1_shift,
        g_qkv,
        g_qv_bias,
        g_out,
        g_out_bias,
        g_ln2_gain,
        g_ln2_shift,
        g_up,
        g_up_bias,
        g_down,
        g_down_bias,
    )


def solution(mesh):
    placed = (
        P("dp", None),
        P("dp", None),
        P(),
        P(),
        P(None, None, "tensor"),
        P(None, "tensor"),
        P("tensor", None),
        P(),
        P(),
        P(),
        P(None, "tensor"),
        P("tensor"),
        P("tensor", None),
        P(),
        P("dp", None),
    )
    return jax.shard_map(
        per_device,
        mesh=mesh,
        in_specs=placed,
        out_specs=(
            P("dp", None),
            P("dp", None),
            P(),
            P(),
            P(None, None, "tensor"),
            P(None, "tensor"),
            P("tensor", None),
            P(),
            P(),
            P(),
            P(None, "tensor"),
            P("tensor"),
            P("tensor", None),
            P(),
        ),
        check_vma=False,
    )
```

profile of v0, /device:TPU:0, one launch (start us, length us, event | category | flops | bytes accessed | tf_op | source)
XLA Modules:
  0.0 623.6 jit_solution(2085231049071354112)
XLA Ops:
  8.2 2.3 convert_reduce_fusion
  13.0 2.6 add_convert_fusion.4
  18.5 2.3 exponential_reduce_fusion
  25.6 2.5 exponential_reduce_fusion.1
  34.1 72.3 %all-reduce.9.cloned.1.call-done = bf16[1024,1024]{1,0:T(8,128)(2,1)} async-done(((bf16[1024,1024]{1,0:T(8,128)(2,1)}), bf16[1024,1024]{1,0:T(8,128)(2,1)}) %all-reduce.9.cloned.1.call-update) | async-done | bytes 2097168 | tf_op jit(solution)/shard_map/psum | solution.py:154
  106.4 3.1 fusion.15
  112.6 2.4 fusion.30
  115.7 4.9 convert_reduce_fusion.1
  121.9 3.7 convolution_convert_fusion
  125.9 6.3 %convolution_convert_fusion.1 = bf16[1024,1024]{1,0:T(8,128)(2,1)} fusion(bf16[1024,1024]{1,0:T(8,128)(2,1)S(1)} %copy-done, f32[1024,1024]{1,0:T(8,128)} %copy-done.41, f32[1024]{0:T(1024)S(1)} %copy-done.38), kind=kOutput, calls=%fused_computation.53 | convolution fusion | flops 2159017984 | bytes 8392704 | tf_op jit(solution)/shard_map/dot_general | solution.py:160
  132.2 63.1 %all-reduce.11.cloned.1.call-done = bf16[1024,1024]{1,0:T(8,128)(2,1)} async-done(((bf16[1024,1024]{1,0:T(8,128)(2,1)}), bf16[1024,1024]{1,0:T(8,128)(2,1)}) %all-reduce.11.cloned.1.call-update) | async-done | bytes 2097168 | tf_op jit(solution)/shard_map/psum | solution.py:172
  195.3 3.8 multiply_reduce_fusion.6
  199.1 3.7 multiply_add_fusion.1
  205.7 3.3 fusion.37
  209.0 3.2 multiply_reduce_fusion
  212.1 5.4 multiply_reduce_fusion.1
  217.5 9.7 %multiply_convert_fusion = (bf16[4,512,1024]{2,1,0:T(8,128)(2,1)}, bf16[4,512,1024]{2,1,0:T(8,128)(2,1)}) fusion(f32[4,512,1024]{2,1,0:T(8,128)S(1)} %get-tuple-element.70, f32[4,512,1024]{2,1,0:T(8,128)S(1)} %bitcast.76, f32[4,512]{1,0:T(4,128)S(1)} %get-tuple-element.69, f32[4,512]{1,0:T(4,128)S(1)} %log_add_fusion, ...), kind=kLoop, calls=%fused_computation | loop fusion | flops 25165824 | bytes 43024384 | tf_op jit(solution)/shard_map/convert_element_type | solution.py:98
  227.2 3.8 fusion.24
  232.2 2.4 fusion.22
  239.5 3.2 bitcast_convert_fusion
  243.0 7.3 %fusion.29 = f32[1024,1024]{1,0:T(8,128)} fusion(bf16[1024,1024]{1,0:T(8,128)(2,1)} %copy-done.43, f32[1024,1024]{1,0:T(8,128)} %copy-done.9, f32[1024]{0:T(1024)S(1)} %copy-done.37, f32[1024]{0:T(1024)S(1)} %copy-done.32), kind=kOutput, calls=%fused_computation.81 | convolution fusion | flops 2150629376 | bytes 10493952 | tf_op jit(solution)/shard_map/sd,sf->df/dot_general | solution.py:169
  250.3 5.1 fusion.52
  257.8 3.6 convolution_bitcast_fusion
  261.5 4.0 convert_element_type.118
  268.4 4.0 convert_element_type.121
  272.4 17.1 %all-reduce.1 = (f32[2,256]{1,0:T(2,128)}, f32[1024]{0:T(1024)}) all-reduce(f32[2,256]{1,0:T(2,128)S(1)} %pad_maximum_fusion.3, f32[1024]{0:T(1024)S(1)} %get-tuple-element.71), channel_id=1, replica_groups=mesh['dp'=8,'tensor'=4] {'dp'}, use_global_device_ids=true, to_apply=%region_25.26 | all-reduce | flops 1536 | bytes 12288 | tf_op jit(solution)/shard_map/psum | solution.py:206
  292.7 53.8 %all-reduce.15.cloned.1.call-done = (bf16[1024,1024]{1,0:T(8,128)(2,1)}, bf16[1024,1024]{1,0:T(8,128)(2,1)}) async-done(((bf16[1024,1024]{1,0:T(8,128)(2,1)}, bf16[1024,1024]{1,0:T(8,128)(2,1)}), (bf16[1024,1024]{1,0:T(8,128)(2,1)}, bf16[1024,1024]{1,0:T(8,128)(2,1)})) %all-reduce.15.cloned.1.call-update) | async-done | bytes 4194320 | tf_op jit(solution)/shard_map/psum | solution.py:161
  350.7 41.5 %all-reduce = (f32[1024]{0:T(1024)}, f32[1024]{0:T(1024)}, f32[1024]{0:T(1024)}, f32[1024]{0:T(1024)}, f32[1024]{0:T(1024)}, /*index=5*/f32[1024]{0:T(1024)}) all-reduce(f32[1024]{0:T(1024)S(1)} %get-tuple-element.31, f32[1024]{0:T(1024)S(1)} %get-tuple-element.30, ...), channel_id=1, replica_groups=mesh['dp'=8,'tensor'=4] {'dp','tensor'}, use_global_device_ids=true, to_apply=%region_19.20 | all-reduce | flops 6144 | bytes 49152 | tf_op jit(solution)/shard_map/psum | solution.py:209
  392.2 6.7 %add_convert_fusion = (bf16[1024,1024]{1,0:T(8,128)(2,1)}, bf16[1024,1024]{1,0:T(8,128)(2,1)}) fusion(f32[1024,1024]{1,0:T(8,128)} %copy-done.5, bf16[1024,1024]{1,0:T(8,128)(2,1)} %get-tuple-element.51, f32[1024]{0:T(1024)S(1)} %broadcast_multiply_fusion, f32[1024]{0:T(1024)S(1)} %broadcast_multiply_fusion.1, f32[1024]{0:T(1024)S(1)} %copy-done.30, ...), kind=kLoop, calls=%fused_computation.32 | loop fusion | flops 18874368 | bytes 16805888 | tf_op jit(solution)/shard_map/convert_element_type | solution.py:199
  398.8 206.4 %all-reduce.13.cloned.1.call-done = (f32[3,1024,256]{1,2,0:T(8,128)}, f32[256,1024]{1,0:T(8,128)}, f32[1024,1024]{1,0:T(8,128)}, f32[1024,1024]{1,0:T(8,128)}) async-done(((f32[3,1024,256]{1,2,0:T(8,128)}, f32[256,1024]{1,0:T(8,128)}, f32[1024,1024]{1,0:T(8,128)}, f32[1024,1024]{1,0:T(8,128)}), (f32[3,1024,256]{1,2,0:T(8,128)}, f32[256,1024]{1,0:T(8,128)}, f32[1024,1024]{1,0:T(8,128)}, ...) | async-done | bytes 12582928 | tf_op jit(solution)/shard_map/psum | solution.py:206
  605.3 3.6 copy.31
  609.9 4.9 copy.43
  (151 shorter events, 47.1 us)
Async XLA Ops:
  7.2 107.8 %copy-start = (bf16[1024,1024]{1,0:T(8,128)(2,1)S(1)}, bf16[1024,1024]{1,0:T(8,128)(2,1)}, u32[]{:S(2)}) copy-start(bf16[1024,1024]{1,0:T(8,128)(2,1)} %param.27) | copy-start | bytes 6291460
  7.2 5.6 copy-start.31
  7.2 5.7 copy-start.30
  7.2 5.7 copy-start.39
  7.2 99.2 %all-reduce.9.cloned.1.call-start = ((), (), s32[]{:S(2)}) async-start(), calls=%async_computation | async-start | bytes 4194304 | tf_op jit(solution)/shard_map/psum | solution.py:154
  7.3 5.7 copy-start.2
  7.3 5.7 copy-start.35
  15.6 12.6 %copy-start.24 = (bf16[1024,3,256]{0,2,1:T(8,128)(2,1)}, bf16[1024,3,256]{0,2,1:T(8,128)(2,1)S(1)}, u32[]{:S(2)}) copy-start(bf16[1024,3,256]{0,2,1:T(8,128)(2,1)S(1)} %add_convert_fusion.4) | copy-start | bytes 4718596
  15.7 8.3 %copy-start.20 = (bf16[4,1024,64]{1,2,0:T(8,128)(2,1)}, bf16[4,1024,64]{1,2,0:T(8,128)(2,1)S(1)}, u32[]{:S(2)}) copy-start(bf16[4,1024,64]{1,2,0:T(8,128)(2,1)S(1)} %slice_bitcast_fusion.2) | copy-start | bytes 1572868
  31.1 75.3 %copy-start.29 = (f32[1024]{0:T(1024)S(1)}, f32[1024]{0:T(1024)}, u32[]{:S(2)}) copy-start(f32[1024]{0:T(1024)} %param.22) | copy-start | bytes 12292
  34.1 161.2 %all-reduce.11.cloned.1.call-start = ((), (), s32[]{:S(2)}) async-start(), calls=%async_computation.1 | async-start | bytes 4194304 | tf_op jit(solution)/shard_map/psum | solution.py:172
  106.4 3.5 copy-start.10
  115.7 4.9 copy-start.41
  125.6 220.9 %all-reduce.15.cloned.1.call-start = ((), (), s32[]{:S(2)}) async-start(), calls=%async_computation.3 | async-start | bytes 8388608 | tf_op jit(solution)/shard_map/psum | solution.py:161
  195.2 3.8 copy-start.14
  195.2 10.4 %slice-start.2 = ((s8[8388608]{0:T(1024)(128)(4,1)}), s8[4194304]{0:T(1024)(128)(4,1)S(1)}, s32[]{:S(2)}) async-start(s8[8388608]{0:T(1024)(128)(4,1)} %bitcast.77), calls=%async_computation.6 | async-start | bytes 8388608
  199.1 5.7 copy-start.23
  199.1 6.5 %slice-start.3 = ((s8[8388608]{0:T(1024)(128)(4,1)}), s8[4194304]{0:T(1024)(128)(4,1)S(1)}, s32[]{:S(2)}) async-start(s8[8388608]{0:T(1024)(128)(4,1)} %bitcast.77), calls=%async_computation.7 | async-start | bytes 8388608
  204.8 4.1 slice-start
  205.6 3.3 slice-start.1
  205.6 3.3 copy-start.25
  227.2 3.8 copy-start.12
  227.2 3.8 copy-start.21
  242.7 7.6 %copy-start.16 = (bf16[1024,1024]{1,0:T(8,128)(2,1)S(1)}, bf16[1024,1024]{1,0:T(8,128)(2,1)}, u32[]{:S(2)}) copy-start(bf16[1024,1024]{1,0:T(8,128)(2,1)} %param.29) | copy-start | bytes 6291460
  242.7 362.5 %all-reduce.13.cloned.1.call-start = ((), (), s32[]{:S(2)}) async-start(), calls=%async_computation.2 | async-start | bytes 25165824 | tf_op jit(solution)/shard_map/psum | solution.py:206
  243.0 7.3 %copy-start.42 = (f32[1024,1024]{1,0:T(8,128)S(1)}, f32[1024,1024]{1,0:T(8,128)}, u32[]{:S(2)}) copy-start(f32[1024,1024]{1,0:T(8,128)} %copy-done.41) | copy-start | bytes 12582916
  250.3 5.1 copy-start.6
  250.3 5.1 copy-start.18
  348.7 43.5 %copy-start.33 = (f32[1024]{0:T(1024)S(1)}, f32[1024]{0:T(1024)}, u32[]{:S(2)}) copy-start(f32[1024]{0:T(1024)} %param.28) | copy-start | bytes 12292
  605.3 3.6 copy-start.28
  609.9 4.9 copy-start.19
  609.9 7.0 %copy-start.1 = (bf16[1024,1024]{1,0:T(8,128)(2,1)S(1)}, bf16[1024,1024]{1,0:T(8,128)(2,1)}, u32[]{:S(2)}) copy-start(bf16[1024,1024]{1,0:T(8,128)(2,1)} %param.27) | copy-start | bytes 6291460
  (20 other events, 43.4 us)
Sparse Core Ops, SparseCore 0:
  34.2 72.1 all-reduce.8
  125.7 69.4 all-reduce.10
  242.8 103.6 all-reduce.14
  349.5 255.6 all-reduce.12
where the time goes:
time: 632 us; the launch traced here: 624 us
  waiting for transfers between devices  396 us (63%)
  matrix products  72.4 us (11%)
  other arithmetic  59.1 us (9%)
  blocking collectives  58.6 us (9%)
  local copies, waits for them, and re-layouts  22.6 us (4%)
  between operations  14.6 us (2%)
    psum x1, waiting for transfers between devices, per_device(): lax.psum((g_qkv, g_qv_bias, g_out, g_up, g_up_bias, g_down), 'dp')  206 us
    psum x1, waiting for transfers between devices, per_device(): lax.psum(attn_part.astype(jnp.bfloat16), 'tensor').astype(jnp.float32)  72.3 us
    psum x1, waiting for transfers between devices, per_device(): lax.psum(normed_part.astype(jnp.bfloat16), 'tensor').astype(jnp.float32)  63.1 us
    psum x1, waiting for transfers between devices, per_device(): lax.psum(mlp_part.astype(jnp.bfloat16), 'tensor').astype(jnp.float32)  53.8 us
    psum x1, blocking collectives, per_device(): lax.psum((g_ln1_gain, g_ln1_shift, g_out_bias, g_ln2_gain, g_ln2_shift, g...  41.5 us
    unnamed x100, local copies, waits for them, and re-layouts  21.5 us
    psum x1, blocking collectives, per_device(): lax.psum((g_qkv, g_qv_bias, g_out, g_up, g_up_bias, g_down), 'dp')  17.1 us
  transfers between devices with their start and end apart: 4, of which 4 were waited for; matrix products, arithmetic and copies ran while one was open for 8% of the time, Pallas kernels for 0%

commit v1 on v0

--- a/solution.py
+++ b/solution.py
@@ -2,10 +2,15 @@
 import jax.numpy as jnp
 from jax import lax
 from jax.sharding import PartitionSpec as P
+from jax.lax import all_gather
 
 HD = 64
 epsilon = 1e-05
 gelu_coef = 0.7978845608028654
+
+
+def _part_ports(array_in, mesh_name):
+    return all_gather(array_in, mesh_name).sum(axis=0)
 
 
 def gelu_value(values):
@@ -151,7 +156,7 @@
     context_heads, log_totals = attention_forward(query_heads, key_heads, value_heads, seg_row)
     context = context_heads.transpose(1, 0, 2).reshape(length, local_width)
     attn_part = jnp.dot(context, w_out, preferred_element_type=jnp.float32)
-    attn_sum = lax.psum(attn_part.astype(jnp.bfloat16), "tensor").astype(jnp.float32)
+    attn_sum = _part_ports(attn_part.astype(jnp.bfloat16), "tensor").astype(jnp.float32)
     resid_mid = tokens_f + attn_sum + b_out
     normed2, inverse2 = norm_parts(resid_mid)
     input2 = (normed2 * ln2_gain + ln2_shift).astype(jnp.bfloat16)

time: 632 us -> 658 us (1.041)
  waiting for transfers between devices: 396 us -> 414 us
  other arithmetic: 59.1 us -> 66.6 us
    all_gather x0 -> x1, waiting for transfers between devices: none -> 90.3 us  [_part_ports(): return all_gather(array_in, mesh_name).sum(axis=0)]
    psum x1 -> x0, waiting for transfers between devices: 72.3 us -> none  [per_device(): lax.psum(attn_part.astype(jnp.bfloat16), 'tensor').astype(jnp.float32)]
    reduce_sum x0 -> x1, other arithmetic: none -> 7.44 us  [_part_ports(): return all_gather(array_in, mesh_name).sum(axis=0)]
where the time goes in v1:
time: 658 us; the launch traced here: 650 us
  waiting for transfers between devices  414 us (63%)
  matrix products  72.9 us (11%)
  other arithmetic  66.6 us (10%)
  blocking collectives  58.7 us (9%)
  local copies, waits for them, and re-layouts  22.6 us (3%)
  between operations  14.9 us (2%)
    psum x1, waiting for transfers between devices, per_device(): lax.psum((g_qkv, g_qv_bias, g_out, g_up, g_up_bias, g_down), 'dp')  206 us
    all_gather x1, waiting for transfers between devices, _part_ports(): return all_gather(array_in, mesh_name).sum(axis=0)  90.3 us
    psum x1, waiting for transfers between devices, per_device(): lax.psum(normed_part.astype(jnp.bfloat16), 'tensor').astype(jnp.float32)  63.2 us
    psum x1, waiting for transfers between devices, per_device(): lax.psum(mlp_part.astype(jnp.bfloat16), 'tensor').astype(jnp.float32)  53.8 us
    psum x1, blocking collectives, per_device(): lax.psum((g_ln1_gain, g_ln1_shift, g_out_bias, g_ln2_gain, g_ln2_shift, g...  41.5 us
    unnamed x100, local copies, waits for them, and re-layouts  21.4 us
    psum x1, blocking collectives, per_device(): lax.psum((g_qkv, g_qv_bias, g_out, g_up, g_up_bias, g_down), 'dp')  17.1 us
  transfers between devices with their start and end apart: 4, of which 4 were waited for; matrix products, arithmetic and copies ran while one was open for 8% of the time, Pallas kernels for 0%

profile of v1, /device:TPU:0, one launch (start us, length us, event | category | flops | bytes accessed | tf_op | source)
XLA Modules:
  0.0 649.7 jit_solution(14629066574958607265)
XLA Ops:
  13.0 2.6 add_convert_fusion.4
  18.5 2.3 exponential_reduce_fusion
  25.6 2.5 exponential_reduce_fusion.1
  34.1 90.3 %all-gather.3.cloned.1.call-done = bf16[4096,1024]{1,0:T(8,128)(2,1)} async-done(((bf16[1024,1024]{1,0:T(8,128)(2,1)}), bf16[4096,1024]{1,0:T(8,128)(2,1)}) %all-gather.3.cloned.1.call-update) | async-done | bytes 8388624 | tf_op jit(solution)/shard_map/all_gather | solution.py:13
  124.4 7.4 %reduce_sum.205 = bf16[1024,1024]{1,0:T(8,128)(2,1)} reduce(bf16[4,1024,1024]{2,1,0:T(8,128)(2,1)} %bitcast.80, bf16[]{:T(256)} %constant.13.clone.1), dimensions={0}, to_apply=%region_6.7 | reduce | flops 3145728 | bytes 10485762 | tf_op jit(solution)/shard_map/reduce_sum | solution.py:13
  131.9 3.1 fusion.15
  138.0 2.4 fusion.30
  141.1 5.3 convert_reduce_fusion.1
  147.7 3.7 convolution_convert_fusion
  151.5 6.4 convolution_convert_fusion.1
  157.9 63.2 %all-reduce.8.cloned.1.call-done = bf16[1024,1024]{1,0:T(8,128)(2,1)} async-done(((bf16[1024,1024]{1,0:T(8,128)(2,1)}), bf16[1024,1024]{1,0:T(8,128)(2,1)}) %all-reduce.8.cloned.1.call-update) | async-done | bytes 2097168 | tf_op jit(solution)/shard_map/psum | solution.py:177
  221.1 3.8 multiply_reduce_fusion.6
  225.0 3.9 multiply_add_fusion.1
  231.7 3.3 fusion.37
  235.0 3.2 multiply_reduce_fusion
  238.1 5.4 multiply_reduce_fusion.1
  243.5 9.5 %multiply_convert_fusion = (bf16[4,512,1024]{2,1,0:T(8,128)(2,1)}, bf16[4,512,1024]{2,1,0:T(8,128)(2,1)}) fusion(f32[4,512,1024]{2,1,0:T(8,128)S(1)} %get-tuple-element.70, f32[4,512,1024]{2,1,0:T(8,128)S(1)} %bitcast.77, f32[4,512]{1,0:T(4,128)S(1)} %get-tuple-element.69, f32[4,512]{1,0:T(4,128)S(1)} %log_add_fusion, ...), kind=kLoop, calls=%fused_computation | loop fusion | flops 25165824 | bytes 43024384 | tf_op jit(solution)/shard_map/convert_element_type | solution.py:103
  253.0 3.8 fusion.24
  258.0 2.4 fusion.22
  265.3 3.2 bitcast_convert_fusion
  268.9 7.3 %fusion.29 = f32[1024,1024]{1,0:T(8,128)} fusion(bf16[1024,1024]{1,0:T(8,128)(2,1)} %copy-done.43, f32[1024,1024]{1,0:T(8,128)} %copy-done.10, f32[1024]{0:T(1024)S(1)} %copy-done.37, f32[1024]{0:T(1024)S(1)} %copy-done.32), kind=kOutput, calls=%fused_computation.81 | convolution fusion | flops 2150629376 | bytes 10493952 | tf_op jit(solution)/shard_map/sd,sf->df/dot_general | solution.py:174
  276.2 5.1 fusion.52
  283.7 3.6 convolution_bitcast_fusion
  287.4 4.0 convert_element_type.120
  294.3 4.0 convert_element_type.123
  298.3 17.1 %all-reduce.1 = (f32[2,256]{1,0:T(2,128)}, f32[1024]{0:T(1024)}) all-reduce(f32[2,256]{1,0:T(2,128)S(1)} %pad_maximum_fusion.3, f32[1024]{0:T(1024)S(1)} %get-tuple-element.71), channel_id=1, replica_groups=mesh['dp'=8,'tensor'=4] {'dp'}, use_global_device_ids=true, to_apply=%region_25.26 | all-reduce | flops 1536 | bytes 12288 | tf_op jit(solution)/shard_map/psum | solution.py:211
  318.5 53.8 %all-reduce.12.cloned.1.call-done = (bf16[1024,1024]{1,0:T(8,128)(2,1)}, bf16[1024,1024]{1,0:T(8,128)(2,1)}) async-done(((bf16[1024,1024]{1,0:T(8,128)(2,1)}, bf16[1024,1024]{1,0:T(8,128)(2,1)}), (bf16[1024,1024]{1,0:T(8,128)(2,1)}, bf16[1024,1024]{1,0:T(8,128)(2,1)})) %all-reduce.12.cloned.1.call-update) | async-done | bytes 4194320 | tf_op jit(solution)/shard_map/psum | solution.py:166
  376.5 41.5 %all-reduce = (f32[1024]{0:T(1024)}, f32[1024]{0:T(1024)}, f32[1024]{0:T(1024)}, f32[1024]{0:T(1024)}, f32[1024]{0:T(1024)}, /*index=5*/f32[1024]{0:T(1024)}) all-reduce(f32[1024]{0:T(1024)S(1)} %get-tuple-element.31, f32[1024]{0:T(1024)S(1)} %get-tuple-element.30, ...), channel_id=1, replica_groups=mesh['dp'=8,'tensor'=4] {'dp','tensor'}, use_global_device_ids=true, to_apply=%region_19.20 | all-reduce | flops 6144 | bytes 49152 | tf_op jit(solution)/shard_map/psum | solution.py:214
  418.1 6.7 %add_convert_fusion = (bf16[1024,1024]{1,0:T(8,128)(2,1)}, bf16[1024,1024]{1,0:T(8,128)(2,1)}) fusion(f32[1024,1024]{1,0:T(8,128)} %copy-done.5, bf16[1024,1024]{1,0:T(8,128)(2,1)} %get-tuple-element.51, f32[1024]{0:T(1024)S(1)} %broadcast_multiply_fusion, f32[1024]{0:T(1024)S(1)} %broadcast_multiply_fusion.1, f32[1024]{0:T(1024)S(1)} %copy-done.30, ...), kind=kLoop, calls=%fused_computation.32 | loop fusion | flops 18874368 | bytes 16805888 | tf_op jit(solution)/shard_map/convert_element_type | solution.py:204
  424.8 206.3 %all-reduce.10.cloned.1.call-done = (f32[3,1024,256]{1,2,0:T(8,128)}, f32[256,1024]{1,0:T(8,128)}, f32[1024,1024]{1,0:T(8,128)}, f32[1024,1024]{1,0:T(8,128)}) async-done(((f32[3,1024,256]{1,2,0:T(8,128)}, f32[256,1024]{1,0:T(8,128)}, f32[1024,1024]{1,0:T(8,128)}, f32[1024,1024]{1,0:T(8,128)}), (f32[3,1024,256]{1,2,0:T(8,128)}, f32[256,1024]{1,0:T(8,128)}, f32[1024,1024]{1,0:T(8,128)}, ...) | async-done | bytes 12582928 | tf_op jit(solution)/shard_map/psum | solution.py:211
  631.1 3.6 copy.31
  635.7 4.9 copy.42
  (152 shorter events, 49.2 us)
Async XLA Ops:
  7.2 133.2 %copy-start = (bf16[1024,1024]{1,0:T(8,128)(2,1)S(1)}, bf16[1024,1024]{1,0:T(8,128)(2,1)}, u32[]{:S(2)}) copy-start(bf16[1024,1024]{1,0:T(8,128)(2,1)} %param.27) | copy-start | bytes 6291460
  7.2 5.6 copy-start.31
  7.2 5.7 copy-start.30
  7.2 5.7 copy-start.39
  7.2 117.2 %all-gather.3.cloned.1.call-start = ((), (), s32[]{:S(2)}) async-start(), calls=%async_computation.1 | async-start | bytes 10485760 | tf_op jit(solution)/shard_map/all_gather | solution.py:13
  7.3 5.7 copy-start.2
  7.3 5.7 copy-start.35
  15.6 12.6 %copy-start.24 = (bf16[1024,3,256]{0,2,1:T(8,128)(2,1)}, bf16[1024,3,256]{0,2,1:T(8,128)(2,1)S(1)}, u32[]{:S(2)}) copy-start(bf16[1024,3,256]{0,2,1:T(8,128)(2,1)S(1)} %add_convert_fusion.4) | copy-start | bytes 4718596
  15.7 8.3 %copy-start.20 = (bf16[4,1024,64]{1,2,0:T(8,128)(2,1)}, bf16[4,1024,64]{1,2,0:T(8,128)(2,1)S(1)}, u32[]{:S(2)}) copy-start(bf16[4,1024,64]{1,2,0:T(8,128)(2,1)S(1)} %slice_bitcast_fusion.2) | copy-start | bytes 1572868
  34.1 187.0 %all-reduce.8.cloned.1.call-start = ((), (), s32[]{:S(2)}) async-start(), calls=%async_computation | async-start | bytes 4194304 | tf_op jit(solution)/shard_map/psum | solution.py:177
  124.4 7.4 %copy-start.29 = (f32[1024]{0:T(1024)S(1)}, f32[1024]{0:T(1024)}, u32[]{:S(2)}) copy-start(f32[1024]{0:T(1024)} %param.22) | copy-start | bytes 12292
  131.9 3.5 copy-start.9
  141.1 5.3 copy-start.41
  151.5 220.9 %all-reduce.12.cloned.1.call-start = ((), (), s32[]{:S(2)}) async-start(), calls=%async_computation.3 | async-start | bytes 8388608 | tf_op jit(solution)/shard_map/psum | solution.py:166
  221.1 3.8 copy-start.14
  221.1 10.5 %slice-start.2 = ((s8[8388608]{0:T(1024)(128)(4,1)}), s8[4194304]{0:T(1024)(128)(4,1)S(1)}, s32[]{:S(2)}) async-start(s8[8388608]{0:T(1024)(128)(4,1)} %bitcast.78), calls=%async_computation.6 | async-start | bytes 8388608
  224.9 5.9 copy-start.23
  225.0 6.7 %slice-start.3 = ((s8[8388608]{0:T(1024)(128)(4,1)}), s8[4194304]{0:T(1024)(128)(4,1)S(1)}, s32[]{:S(2)}) async-start(s8[8388608]{0:T(1024)(128)(4,1)} %bitcast.78), calls=%async_computation.7 | async-start | bytes 8388608
  230.9 4.1 slice-start
  231.6 3.3 slice-start.1
  231.7 3.3 copy-start.25
  253.0 3.8 copy-start.12
  253.0 3.8 copy-start.21
  268.5 7.6 %copy-start.16 = (bf16[1024,1024]{1,0:T(8,128)(2,1)S(1)}, bf16[1024,1024]{1,0:T(8,128)(2,1)}, u32[]{:S(2)}) copy-start(bf16[1024,1024]{1,0:T(8,128)(2,1)} %param.29) | copy-start | bytes 6291460
  268.5 362.6 %all-reduce.10.cloned.1.call-start = ((), (), s32[]{:S(2)}) async-start(), calls=%async_computation.2 | async-start | bytes 25165824 | tf_op jit(solution)/shard_map/psum | solution.py:211
  268.8 7.3 %copy-start.42 = (f32[1024,1024]{1,0:T(8,128)S(1)}, f32[1024,1024]{1,0:T(8,128)}, u32[]{:S(2)}) copy-start(f32[1024,1024]{1,0:T(8,128)} %copy-done.41) | copy-start | bytes 12582916
  276.2 5.1 copy-start.6
  276.2 5.1 copy-start.18
  374.6 43.5 %copy-start.33 = (f32[1024]{0:T(1024)S(1)}, f32[1024]{0:T(1024)}, u32[]{:S(2)}) copy-start(f32[1024]{0:T(1024)} %param.28) | copy-start | bytes 12292
  631.1 3.6 copy-start.28
  635.7 4.9 copy-start.19
  635.7 7.0 %copy-start.1 = (bf16[1024,1024]{1,0:T(8,128)(2,1)S(1)}, bf16[1024,1024]{1,0:T(8,128)(2,1)}, u32[]{:S(2)}) copy-start(bf16[1024,1024]{1,0:T(8,128)(2,1)} %param.27) | copy-start | bytes 6291460
  (20 other events, 43.4 us)
Sparse Core Ops, SparseCore 0:
  34.2 90.1 all-gather.2
  151.6 69.4 all-reduce.7
  268.6 103.6 all-reduce.11
  375.4 255.6 all-reduce.9
